TPU v7x, 32 devices: a whole 2x2x4 slice. The times are simulated.
32 devices in a mesh: blk: 8 (over z, core), col: 4 (over y, x).
Axes of the slice: x: 2, y: 2, z: 4, core: 2. Of those that a mesh axis runs over, the one named last changes fastest.
Arguments:
- stiffness: bfloat16 [64, 3, 128, 128], P('blk'), may hold values from -0.3125 to 0.3125
- block_cols: int32 [64, 3], P('blk'), may hold values from 0 to 63, as said below
- basis: bfloat16 [8192, 3, 512], P('blk', None, 'col'), may hold values from -1.1953125 to 1.1953125
- patch_reach: int32 [8, 512, 2], P(None, 'col'), may hold values from 0 to 8
Outputs:
- coarse: float32 [4096, 5, 512], P(('blk', 'col'))
Inputs may be any that keep to these rules, and one draw needn't show every extreme that they name: `block_cols`: block row b lists block row b first and then two other distinct block rows among b - 2 .. b + 2 (periodic); the first block row of each slab lists b - 2 and b + 2.
All inputs are finite; a program needn't handle non-finite values.
Results may differ from a plain program's by a relative error of at most 0.0029.
Values may be sent and summed in bfloat16 or wider, within the bound.
No kernel may reach another device: no remote copies, remote signals or barrier semaphores. Data moves between devices by JAX's collectives and lax.ppermute only.
A program may use at most 64 MiB of HBM per device.

v0:
```python
import jax
import jax.numpy as jnp
from jax import lax
from jax.sharding import PartitionSpec as P


def extended_2(array, sides, width):
    for axis, dim in sides:
        peers, length = (lax.axis_size(axis), array.shape[dim])
        up = [(i, (i + 1) % peers) for i in range(peers)]
        down = [(j, i) for i, j in up]
        last = lax.slice_in_dim(array, length - width, length, axis=dim)
        leading = lax.slice_in_dim(array, 0, width, axis=dim)
        before = lax.ppermute(last, axis, up)
        after = lax.ppermute(leading, axis, down)
        array = jnp.concatenate([before, array, after], axis=dim)
    return array


def shifted(value, axis, steps):
    count = lax.axis_size(axis)
    pairs = [(source, (source + steps) % count) for source in range(count)]
    return lax.ppermute(value, axis, pairs)


def place_tile(tile, offset_pos):
    return jnp.pad(tile, ((0, 0), (offset_pos, 2 - offset_pos), (0, 0)))


def shards(stiffness, block_cols, basis, patch_reach):
    blocks = stiffness.shape[0]
    block_size = stiffness.shape[2]
    row_count = basis.shape[0]
    groups = basis.shape[1]
    local_cols = basis.shape[2]
    slab_count = lax.axis_size("blk")
    slab_index = lax.axis_index("blk")
    total_blocks = blocks * slab_count
    reach_low = lax.dynamic_index_in_dim(patch_reach, (slab_index - 1) % slab_count, 0, False)
    reach_high = lax.dynamic_index_in_dim(patch_reach, (slab_index + 1) % slab_count, 0, False)
    block_row = jnp.arange(row_count, dtype=jnp.int32) // block_size
    lower_mask = block_row[:, None] < reach_low[None, :, 1]
    upper_mask = block_row[:, None] >= blocks - reach_high[None, :, 0]
    support = jnp.stack([lower_mask, jnp.ones_like(lower_mask), upper_mask], 1)
    masked = jnp.where(support, basis, jnp.zeros_like(basis))
    rim_width = 2 * block_size
    padded = extended_2(masked, (("blk", 0),), rim_width)
    zero_rim = jnp.zeros((rim_width, 1, local_cols), masked.dtype)
    lower_rim = jnp.concatenate([padded[:rim_width, 1:], zero_rim], 1)
    upper_rim = jnp.concatenate([zero_rim, padded[rim_width + row_count :, :2]], 1)
    extended = jnp.concatenate([lower_rim, masked, upper_rim], 0)
    extended = extended.reshape(blocks + 4, block_size, groups * local_cols)
    position = (block_cols - slab_index * blocks + 2) % total_blocks
    picked = jnp.take(extended, position, axis=0)
    stiff_image = jnp.einsum(
        "rsij,rsjc->ric", stiffness, picked, preferred_element_type=jnp.float32
    )
    stiff_image = stiff_image.astype(jnp.bfloat16).reshape(row_count, groups, local_cols)
    tile_sums = jnp.einsum(
        "rgl,rhc->glhc",
        masked,
        lax.all_gather(stiff_image, "col", axis=2, tiled=True),
        preferred_element_type=jnp.float32,
    )
    from_prev = shifted(tile_sums[2], "blk", 1)
    from_next = shifted(tile_sums[0], "blk", -1)
    return place_tile(from_prev, 0) + place_tile(tile_sums[1], 1) + place_tile(from_next, 2)


def solution(mesh):
    in_specs = (
        P("blk", None, None, None),
        P("blk", None),
        P("blk", None, "col"),
        P(None, "col", None),
    )
    out_specs = P(("blk", "col"), None, None)
    return jax.shard_map(shards, mesh=mesh, in_specs=in_specs, out_specs=out_specs, check_vma=False)
```

profile of v0, /device:TPU:1, one launch (start us, length us, event | category | flops | bytes accessed | tf_op | source)
XLA Modules:
  0.0 118.4 jit_solution(4530870687081001309)
XLA Ops:
  6.5 0.0 copy-start
  6.5 0.0 copy-start.1
  6.5 0.0 all-gather.2.cloned.1.call-start
  6.6 0.1 pad.21.clone
  6.6 0.7 dynamic-slice_bitcast_fusion.1
  7.3 0.2 broadcast_compare_fusion.1
  7.6 1.5 %add_select_fusion = bf16[1024,3,128]{2,0,1:T(8,128)(2,1)S(1)} fusion(bf16[1024,3,128]{2,0,1:T(8,128)(2,1)} %param.6, pred[1024,1,128]{2,0,1:T(8,128)(4,1)S(1)} %get-tuple-element.15, pred[1024,1,128]{2,0,1:T(8,128)(4,1)S(1)} %get-tuple-element.14, pred[3]{0:T(512)(128)(4,1)S(1)} %pad.21.clone), kind=kLoop, calls=%fused_computation.11 | loop fusion | flops 1179648 | bytes 1835011 | tf_op jit(solution)/shard_map/jit(_where)/select_n | solution.py:45
  9.1 2.7 %collective-permute-start = (bf16[256,3,128]{2,0,1:T(8,128)(2,1)S(1)}, bf16[256,3,128]{2,0,1:T(8,128)(2,1)S(1)}, u32[]{:S(2)}, u32[]{:S(2)}) collective-permute-start(bf16[256,3,128]{2,0,1:T(8,128)(2,1)S(1)} %get-tuple-element.10), channel_id=1, source_target_pairs={{0,4},{4,8},{8,12},{12,16},{16,20},{20,24},{24,28},{28,0},{1,5},{5... | collective-permute-start | bytes 589832 | tf_op jit(solution)/shard_map/ppermute | solution.py:14
  11.8 0.0 collective-permute-start.1
  11.8 0.0 copy-done.1
  11.8 0.1 copy.8
  11.9 0.1 copy.10
  12.0 0.1 reshape.126
  12.1 2.3 %collective-permute-done = bf16[256,3,128]{2,0,1:T(8,128)(2,1)S(1)} collective-permute-done((bf16[256,3,128]{2,0,1:T(8,128)(2,1)S(1)}, bf16[256,3,128]{2,0,1:T(8,128)(2,1)S(1)}, u32[]{:S(2)}, u32[]{:S(2)}) %collective-permute-start) | collective-permute-done | bytes 196640 | tf_op jit(solution)/shard_map/ppermute | solution.py:14
  14.4 4.0 %collective-permute-done.1 = bf16[256,3,128]{2,0,1:T(8,128)(2,1)S(1)} collective-permute-done((bf16[256,3,128]{2,0,1:T(8,128)(2,1)S(1)}, bf16[256,3,128]{2,0,1:T(8,128)(2,1)S(1)}, u32[]{:S(2)}, u32[]{:S(2)}) %collective-permute-start.1) | collective-permute-done | bytes 196640 | tf_op jit(solution)/shard_map/ppermute | solution.py:15
  18.4 0.1 fusion.12
  18.5 8.3 %copy.20 = bf16[1536,3,128]{2,1,0:T(4,128)(2,1)} copy(bf16[1536,3,128]{2,0,1:T(8,128)(2,1)S(1)} %fusion.12) | data formatting | bytes 2359296 | tf_op jit(solution)/shard_map/reshape | solution.py:52
  26.8 3.4 %reshape.137 = bf16[12,128,384]{2,1,0:T(8,128)(2,1)S(1)} reshape(bf16[1536,3,128]{2,1,0:T(4,128)(2,1)} %copy.20) | data formatting | bytes 2359296 | tf_op jit(solution)/shard_map/reshape | solution.py:52
  30.2 2.4 %gather_fusion = bf16[24,128,384]{2,1,0:T(8,128)(2,1)} fusion(bf16[12,128,384]{2,1,0:T(8,128)(2,1)S(1)} %reshape.137, s32[1024]{0:T(1024)S(1)} %pad_clamp_fusion), kind=kCustom, calls=%fused_computation | custom fusion | bytes 4718688 | tf_op jit(solution)/shard_map/jit(_take)/gather | solution.py:54
  32.6 4.3 %copy.12 = bf16[8,3,128,384]{2,3,1,0:T(8,128)(2,1)} copy(bf16[8,3,128,384]{3,2,1,0:T(8,128)(2,1)} %bitcast.34) | data formatting | bytes 4718592 | tf_op jit(solution)/shard_map/jit(_take)/gather | solution.py:54
  36.9 0.0 copy-done
  36.9 2.5 %fusion.9 = bf16[8,128,384]{1,2,0:T(8,128)(2,1)S(1)} fusion(bf16[8,3,128,128]{3,2,1,0:T(8,128)(2,1)S(1)} %copy-done, bf16[8,3,128,384]{2,3,1,0:T(8,128)(2,1)} %copy.12, pred[8,3]{1,0:T(8,128)(4,1)S(1)} %copy.8), kind=kOutput, calls=%fused_computation.13 | convolution fusion | flops 303562752 | bytes 3932184 | tf_op jit(solution)/shard_map/rsij,rsjc->ric/dot_general | solution.py:55
  39.4 0.5 copy.13
  39.9 0.3 reshape.123
  40.2 1.2 copy.14
  41.4 0.0 all-gather.2.cloned.1.call-update
  41.4 43.6 %all-gather.2.cloned.1.call-done = bf16[1024,3,512]{2,0,1:T(8,128)(2,1)} async-done(((bf16[1024,3,128]{2,0,1:T(8,128)(2,1)}), bf16[1024,3,512]{2,0,1:T(8,128)(2,1)}) %all-gather.2.cloned.1.call-update) | async-done | bytes 3145744 | tf_op jit(solution)/shard_map/all_gather | solution.py:62
  85.0 3.3 %fusion = f32[3,128,3,512]{3,1,2,0:T(8,128)S(1)} fusion(bf16[1024,3,512]{2,0,1:T(8,128)(2,1)} %all-gather.2.cloned.1.call-done, bf16[1024,3,128]{2,0,1:T(8,128)(2,1)S(1)} %add_select_fusion), kind=kOutput, calls=%fused_computation.1 | convolution fusion | flops 1207959552 | bytes 6291456 | tf_op jit(solution)/shard_map/rgl,rhc->glhc/dot_general | solution.py:59
  88.3 0.2 slice_bitcast_fusion.2
  88.6 1.8 %collective-permute-start.2 = (f32[128,3,512]{2,0,1:T(8,128)S(1)}, f32[128,3,512]{2,0,1:T(8,128)S(1)}, u32[]{:S(2)}, u32[]{:S(2)}) collective-permute-start(f32[128,3,512]{2,0,1:T(8,128)S(1)} %get-tuple-element.7), channel_id=1, source_target_pairs={{0,4},{4,8},{8,12},{12,16},{16,20},{20,24},{24,28},{28,0},{1,5},{5... | collective-permute-start | bytes 2359304 | tf_op jit(solution)/shard_map/ppermute | solution.py:23
  90.4 0.0 collective-permute-start.3
  90.4 14.7 %collective-permute-done.2 = f32[128,3,512]{2,0,1:T(8,128)S(1)} collective-permute-done((f32[128,3,512]{2,0,1:T(8,128)S(1)}, f32[128,3,512]{2,0,1:T(8,128)S(1)}, u32[]{:S(2)}, u32[]{:S(2)}) %collective-permute-start.2) | collective-permute-done | bytes 786464 | tf_op jit(solution)/shard_map/ppermute | solution.py:23
  105.0 5.2 %collective-permute-done.3 = f32[128,3,512]{2,0,1:T(8,128)S(1)} collective-permute-done((f32[128,3,512]{2,0,1:T(8,128)S(1)}, f32[128,3,512]{2,0,1:T(8,128)S(1)}, u32[]{:S(2)}, u32[]{:S(2)}) %collective-permute-start.3) | collective-permute-done | bytes 786464 | tf_op jit(solution)/shard_map/ppermute | solution.py:23
  110.2 1.3 %pad_add_fusion = f32[128,5,512]{2,0,1:T(8,128)} fusion(f32[128,3,512]{2,0,1:T(8,128)S(1)} %collective-permute-done.3, f32[128,3,512]{2,0,1:T(8,128)S(1)} %get-tuple-element.9, f32[128,3,512]{2,0,1:T(8,128)S(1)} %collective-permute-done.2), kind=kLoop, calls=%fused_computation.12 | loop fusion | flops 655360 | bytes 3670016 | tf_op jit(solution)/shard_map/add | solution.py:67
  (7 shorter events, 0.1 us)
Async XLA Ops:
  6.5 30.4 %copy-start = (bf16[8,3,128,128]{3,2,1,0:T(8,128)(2,1)S(1)}, bf16[8,3,128,128]{3,2,1,0:T(8,128)(2,1)}, u32[]{:S(2)}) copy-start(bf16[8,3,128,128]{3,2,1,0:T(8,128)(2,1)} %param.4) | copy-start | bytes 2359300
  6.5 5.3 %copy-start.1 = (s32[8,3]{0,1:T(4,128)S(1)}, s32[8,3]{0,1:T(4,128)}, u32[]{:S(2)}) copy-start(s32[8,3]{0,1:T(4,128)} %param.5) | copy-start | bytes 292
  6.5 78.5 %all-gather.2.cloned.1.call-start = ((), (), s32[]{:S(2)}) async-start(), calls=%async_computation | async-start | bytes 3932160 | tf_op jit(solution)/shard_map/all_gather | solution.py:62
  9.1 5.4 %collective-permute-start = (bf16[256,3,128]{2,0,1:T(8,128)(2,1)S(1)}, bf16[256,3,128]{2,0,1:T(8,128)(2,1)S(1)}, u32[]{:S(2)}, u32[]{:S(2)}) collective-permute-start(bf16[256,3,128]{2,0,1:T(8,128)(2,1)S(1)} %get-tuple-element.10), channel_id=1, source_target_pairs={{0,4},{4,8},{8,12},{12,16},{16,20},{20,24},{24,28},{28,0},{1,5},{5... | collective-permute-start | bytes 589832 | tf_op jit(solution)/shard_map/ppermute | solution.py:14
  11.8 6.6 %collective-permute-start.1 = (bf16[256,3,128]{2,0,1:T(8,128)(2,1)S(1)}, bf16[256,3,128]{2,0,1:T(8,128)(2,1)S(1)}, u32[]{:S(2)}, u32[]{:S(2)}) collective-permute-start(bf16[256,3,128]{2,0,1:T(8,128)(2,1)S(1)} %get-tuple-element.11), channel_id=1, source_target_pairs={{4,0},{8,4},{12,8},{16,12},{20,16},{24,20},{28,24},{0,28},{5,1},{9... | collective-permute-start | bytes 589832 | tf_op jit(solution)/shard_map/ppermute | solution.py:15
  88.6 16.5 %collective-permute-start.2 = (f32[128,3,512]{2,0,1:T(8,128)S(1)}, f32[128,3,512]{2,0,1:T(8,128)S(1)}, u32[]{:S(2)}, u32[]{:S(2)}) collective-permute-start(f32[128,3,512]{2,0,1:T(8,128)S(1)} %get-tuple-element.7), channel_id=1, source_target_pairs={{0,4},{4,8},{8,12},{12,16},{16,20},{20,24},{24,28},{28,0},{1,5},{5... | collective-permute-start | bytes 2359304 | tf_op jit(solution)/shard_map/ppermute | solution.py:23
  90.4 19.8 %collective-permute-start.3 = (f32[128,3,512]{2,0,1:T(8,128)S(1)}, f32[128,3,512]{2,0,1:T(8,128)S(1)}, u32[]{:S(2)}, u32[]{:S(2)}) collective-permute-start(f32[128,3,512]{2,0,1:T(8,128)S(1)} %get-tuple-element.8), channel_id=1, source_target_pairs={{0,28},{4,0},{8,4},{12,8},{16,12},{20,16},{24,20},{28,24},{1,29},{... | collective-permute-start | bytes 2359304 | tf_op jit(solution)/shard_map/ppermute | solution.py:23
Sparse Core Ops, SparseCore 0:
  41.5 43.4 all-gather.1
where the time goes:
time: 119 us; the launch traced here: 118 us
  waiting for transfers between devices  69.8 us (59%)
  local copies, waits for them, and re-layouts  21.6 us (18%)
  between operations  13.5 us (11%)
  matrix products  5.78 us (5%)
  starting transfers between devices  4.56 us (4%)
  other arithmetic  3.1 us (3%)
    all_gather x1, waiting for transfers between devices, shards(): lax.all_gather(stiff_image, 'col', axis=2, tiled=True)  43.6 us
    ppermute x2, waiting for transfers between devices, shifted(): return lax.ppermute(value, axis, pairs)  19.8 us
    reshape x2, local copies, waits for them, and re-layouts, shards(): extended = extended.reshape(blocks + 4, block_size, groups * local_cols)  11.6 us
    gather x2, local copies, waits for them, and re-layouts, shards(): picked = jnp.take(extended, position, axis=0)  6.73 us
    ppermute x1, waiting for transfers between devices, extended_2(): after = lax.ppermute(leading, axis, down)  4 us
    dot_general x1, matrix products, shards(): jnp.einsum('rgl,rhc->glhc', masked, lax.all_gather(stiff_image, 'col', ax...  3.29 us
    ppermute x1, starting transfers between devices, extended_2(): before = lax.ppermute(last, axis, up)  2.74 us
    dot_general x1, matrix products, shards(): jnp.einsum('rsij,rsjc->ric', stiffness, picked, preferred_element_type=jn...  2.48 us
  transfers between devices with their start and end apart: 5, of which 5 were waited for; matrix products, arithmetic and copies ran while one was open for 0% of the time, Pallas kernels for 0%

commit v1 on v0

--- a/solution.py
+++ b/solution.py
@@ -2,6 +2,12 @@
 import jax.numpy as jnp
 from jax import lax
 from jax.sharding import PartitionSpec as P
+
+
+def joined_along(tiles, dim):
+    tiles = jnp.moveaxis(tiles, 0, dim)
+    dims = tiles.shape
+    return tiles.reshape(*dims[:dim], dims[dim] * dims[dim + 1], *dims[dim + 2 :])
 
 
 def extended_2(array, sides, width):
@@ -56,12 +62,26 @@
         "rsij,rsjc->ric", stiffness, picked, preferred_element_type=jnp.float32
     )
     stiff_image = stiff_image.astype(jnp.bfloat16).reshape(row_count, groups, local_cols)
-    tile_sums = jnp.einsum(
-        "rgl,rhc->glhc",
-        masked,
-        lax.all_gather(stiff_image, "col", axis=2, tiled=True),
-        preferred_element_type=jnp.float32,
-    )
+    size, index, rows = (lax.axis_size("col"), lax.axis_index("col"), stiff_image.shape[2])
+    ahead = [(i_2, (i_2 + 1) % size) for i_2 in range(size)]
+    behind = [(i_2, (i_2 - 1) % size) for i_2 in range(size)]
+    half = size // 2
+    pieces = {}
+    from_left = from_right = stiff_image
+    for step in range(half + 1):
+        next_left = lax.ppermute(from_left, "col", ahead) if step < half else None
+        next_right = lax.ppermute(from_right, "col", behind) if step < size - half - 1 else None
+        pieces[-step] = jnp.einsum(
+            "rgl,rhc->glhc", masked, from_left, preferred_element_type=jnp.float32
+        )
+        if 0 < step < size - half:
+            pieces[step] = jnp.einsum(
+                "rgl,rhc->glhc", masked, from_right, preferred_element_type=jnp.float32
+            )
+        from_left, from_right = (next_left, next_right)
+    pieces = jnp.stack([pieces[k] for k in sorted(pieces)])
+    pieces = pieces[(jnp.arange(size) - index + half) % size]
+    tile_sums = joined_along(pieces, 3)
     from_prev = shifted(tile_sums[2], "blk", 1)
     from_next = shifted(tile_sums[0], "blk", -1)
     return place_tile(from_prev, 0) + place_tile(tile_sums[1], 1) + place_tile(from_next, 2)

time: 119 us -> 119 us (level)
  between operations: 13.5 us -> 0.15 us
  local copies, waits for them, and re-layouts: 21.6 us -> 29.5 us
  starting transfers between devices: 4.56 us -> 7.88 us
  waiting for transfers between devices: 69.8 us -> 71 us
    ppermute x0 -> x3, waiting for transfers between devices: none -> 46.8 us  [the longest x2 31.6 us: shards(): next_left = lax.ppermute(from_left, 'col', ahead) if step < half else None]
    all_gather x1 -> x0, waiting for transfers between devices: 43.6 us -> none  [shards(): lax.all_gather(stiff_image, 'col', axis=2, tiled=True)]
    slice x0 -> x4, local copies, waits for them, and re-layouts: none -> 4.37 us  [the longest x2 2.96 us: shards(): from_prev = shifted(tile_sums[2], 'blk', 1)]
    ppermute x0 -> x3, starting transfers between devices: none -> 3.53 us  [the longest x2 2.58 us: shards(): next_left = lax.ppermute(from_left, 'col', ahead) if step < half else None]
    gather x0 -> x1, local copies, waits for them, and re-layouts: none -> 2.13 us  [shards(): pieces = pieces[(jnp.arange(size) - index + half) % size]]
    ppermute x2, waiting for transfers between devices: 19.8 us -> 17.9 us  [shifted(): return lax.ppermute(value, axis, pairs)]
    add x0 -> x1, local copies, waits for them, and re-layouts: none -> 1.46 us  [shards(): place_tile(from_prev, 0) + place_tile(tile_sums[1], 1)]
    dot_general x1 -> x4, matrix products: 3.29 us -> 3.51 us  [the longest x3 1.79 us: shards(): jnp.einsum('rgl,rhc->glhc', masked, from_left, preferred_element_type=jnp...]
  transfers between devices with their start and end apart: 5 -> 7, of which waited for: 5 -> 7; matrix products, arithmetic and copies ran while one was open for 0% -> 4% of each run, Pallas kernels for 0% -> 0%
where the time goes in v1:
time: 119 us; the launch traced here: 118 us
  waiting for transfers between devices  71 us (60%)
  local copies, waits for them, and re-layouts  29.5 us (25%)
  starting transfers between devices  7.88 us (7%)
  matrix products  5.99 us (5%)
  other arithmetic  3.55 us (3%)
    ppermute x2, waiting for transfers between devices, shards(): next_left = lax.ppermute(from_left, 'col', ahead) if step < half else None  31.6 us
    ppermute x2, waiting for transfers between devices, shifted(): return lax.ppermute(value, axis, pairs)  17.9 us
    ppermute x1, waiting for transfers between devices, shards(): lax.ppermute(from_right, 'col', behind)  15.2 us
    reshape x2, local copies, waits for them, and re-layouts, shards(): extended = extended.reshape(blocks + 4, block_size, groups * local_cols)  11.6 us
    gather x2, local copies, waits for them, and re-layouts, shards(): picked = jnp.take(extended, position, axis=0)  6.73 us
    ppermute x1, waiting for transfers between devices, extended_2(): after = lax.ppermute(leading, axis, down)  4 us
    slice x2, local copies, waits for them, and re-layouts, shards(): from_prev = shifted(tile_sums[2], 'blk', 1)  2.96 us
    ppermute x1, starting transfers between devices, extended_2(): before = lax.ppermute(last, axis, up)  2.74 us
  transfers between devices with their start and end apart: 7, of which 7 were waited for; matrix products, arithmetic and copies ran while one was open for 4% of the time, Pallas kernels for 0%

profile of v1, /device:TPU:1, one launch (start us, length us, event | category | flops | bytes accessed | tf_op | source)
XLA Modules:
  0.0 118.1 jit_solution(12272065260451694636)
XLA Ops:
  0.0 0.0 copy-start
  0.0 0.0 copy-start.1
  0.0 0.8 dynamic-slice_bitcast_fusion.1
  0.8 0.1 pad.25.clone
  0.9 0.2 broadcast_compare_fusion.1
  1.1 1.5 %add_select_fusion = bf16[1024,3,128]{2,0,1:T(8,128)(2,1)S(1)} fusion(bf16[1024,3,128]{2,0,1:T(8,128)(2,1)} %param.6, pred[1024,1,128]{2,0,1:T(8,128)(4,1)S(1)} %get-tuple-element.15, pred[1024,1,128]{2,0,1:T(8,128)(4,1)S(1)} %get-tuple-element.14, pred[3]{0:T(512)(128)(4,1)S(1)} %pad.25.clone), kind=kLoop, calls=%fused_computation.11 | loop fusion | flops 1179648 | bytes 1835011 | tf_op jit(solution)/shard_map/jit(_where)/select_n | solution.py:51
  2.6 2.7 %collective-permute-start = (bf16[256,3,128]{2,0,1:T(8,128)(2,1)S(1)}, bf16[256,3,128]{2,0,1:T(8,128)(2,1)S(1)}, u32[]{:S(2)}, u32[]{:S(2)}) collective-permute-start(bf16[256,3,128]{2,0,1:T(8,128)(2,1)S(1)} %get-tuple-element.10), channel_id=1, source_target_pairs={{0,4},{4,8},{8,12},{12,16},{16,20},{20,24},{24,28},{28,0},{1,5},{5... | collective-permute-start | bytes 589832 | tf_op jit(solution)/shard_map/ppermute | solution.py:20
  5.3 0.0 collective-permute-start.1
  5.3 0.0 copy-done.1
  5.4 0.1 copy.13
  5.4 0.1 reshape.185
  5.5 0.1 copy.11
  5.6 2.3 %collective-permute-done = bf16[256,3,128]{2,0,1:T(8,128)(2,1)S(1)} collective-permute-done((bf16[256,3,128]{2,0,1:T(8,128)(2,1)S(1)}, bf16[256,3,128]{2,0,1:T(8,128)(2,1)S(1)}, u32[]{:S(2)}, u32[]{:S(2)}) %collective-permute-start) | collective-permute-done | bytes 196640 | tf_op jit(solution)/shard_map/ppermute | solution.py:20
  8.0 4.0 %collective-permute-done.1 = bf16[256,3,128]{2,0,1:T(8,128)(2,1)S(1)} collective-permute-done((bf16[256,3,128]{2,0,1:T(8,128)(2,1)S(1)}, bf16[256,3,128]{2,0,1:T(8,128)(2,1)S(1)}, u32[]{:S(2)}, u32[]{:S(2)}) %collective-permute-start.1) | collective-permute-done | bytes 196640 | tf_op jit(solution)/shard_map/ppermute | solution.py:21
  12.0 0.1 fusion.10
  12.1 8.3 %copy.36 = bf16[1536,3,128]{2,1,0:T(4,128)(2,1)} copy(bf16[1536,3,128]{2,0,1:T(8,128)(2,1)S(1)} %fusion.10) | data formatting | bytes 2359296 | tf_op jit(solution)/shard_map/reshape | solution.py:58
  20.3 3.4 %reshape.210 = bf16[12,128,384]{2,1,0:T(8,128)(2,1)S(1)} reshape(bf16[1536,3,128]{2,1,0:T(4,128)(2,1)} %copy.36) | data formatting | bytes 2359296 | tf_op jit(solution)/shard_map/reshape | solution.py:58
  23.7 2.4 %gather_fusion = bf16[24,128,384]{2,1,0:T(8,128)(2,1)} fusion(bf16[12,128,384]{2,1,0:T(8,128)(2,1)S(1)} %reshape.210, s32[1024]{0:T(1024)S(1)} %pad_clamp_fusion.1), kind=kCustom, calls=%fused_computation | custom fusion | bytes 4718688 | tf_op jit(solution)/shard_map/jit(_take)/gather | solution.py:60
  26.1 4.3 %copy.15 = bf16[8,3,128,384]{2,3,1,0:T(8,128)(2,1)} copy(bf16[8,3,128,384]{3,2,1,0:T(8,128)(2,1)} %bitcast.61) | data formatting | bytes 4718592 | tf_op jit(solution)/shard_map/jit(_take)/gather | solution.py:60
  30.4 0.0 copy-done
  30.4 2.5 %fusion.7 = bf16[8,128,384]{1,2,0:T(8,128)(2,1)S(1)} fusion(bf16[8,3,128,128]{3,2,1,0:T(8,128)(2,1)S(1)} %copy-done, bf16[8,3,128,384]{2,3,1,0:T(8,128)(2,1)} %copy.15, pred[8,3]{1,0:T(8,128)(4,1)S(1)} %copy.11), kind=kOutput, calls=%fused_computation.13 | convolution fusion | flops 303562752 | bytes 3932184 | tf_op jit(solution)/shard_map/rsij,rsjc->ric/dot_general | solution.py:61
  32.9 0.5 copy.16
  33.4 0.3 reshape.182
  33.8 1.2 copy.17
  34.9 1.7 %collective-permute-start.2 = (bf16[1024,3,128]{2,0,1:T(8,128)(2,1)}, bf16[1024,3,128]{2,0,1:T(8,128)(2,1)S(1)}, u32[]{:S(2)}, u32[]{:S(2)}) collective-permute-start(bf16[1024,3,128]{2,0,1:T(8,128)(2,1)} %copy.17), channel_id=1, source_target_pairs={{0,1},{1,2},{2,3},{3,0},{4,5},{5,6},{6,7},{7,4},{8,9},{9,10},{10,1... | collective-permute-start | bytes 2359304 | tf_op jit(solution)/shard_map/ppermute | solution.py:72
  36.6 1.0 collective-permute-start.4
  37.6 18.0 %collective-permute-done.2 = bf16[1024,3,128]{2,0,1:T(8,128)(2,1)S(1)} collective-permute-done((bf16[1024,3,128]{2,0,1:T(8,128)(2,1)}, bf16[1024,3,128]{2,0,1:T(8,128)(2,1)S(1)}, u32[]{:S(2)}, u32[]{:S(2)}) %collective-permute-start.2) | collective-permute-done | bytes 786464 | tf_op jit(solution)/shard_map/ppermute | solution.py:72
  55.6 0.9 collective-permute-start.3
  56.5 0.6 convolution_bitcast_fusion.1
  57.1 0.6 convolution_bitcast_fusion.2
  57.7 15.2 %collective-permute-done.4 = bf16[1024,3,128]{2,0,1:T(8,128)(2,1)} collective-permute-done((bf16[1024,3,128]{2,0,1:T(8,128)(2,1)}, bf16[1024,3,128]{2,0,1:T(8,128)(2,1)}, u32[]{:S(2)}, u32[]{:S(2)}) %collective-permute-start.4) | collective-permute-done | bytes 786464 | tf_op jit(solution)/shard_map/ppermute | solution.py:73
  73.0 1.7 %convolution_bitcast_fusion = f32[1,3,128,3,128]{4,2,3,1,0:T(8,128)S(1)} fusion(bf16[1024,3,128]{2,0,1:T(8,128)(2,1)S(1)} %add_select_fusion, bf16[1024,3,128]{2,0,1:T(8,128)(2,1)} %collective-permute-done.4), kind=kOutput, calls=%fused_computation.14 | convolution fusion | flops 301989888 | bytes 2162688 | tf_op jit(solution)/shard_map/rgl,rhc->glhc/dot_general | solution.py:78
  74.7 13.6 %collective-permute-done.3 = bf16[1024,3,128]{2,0,1:T(8,128)(2,1)S(1)} collective-permute-done((bf16[1024,3,128]{2,0,1:T(8,128)(2,1)S(1)}, bf16[1024,3,128]{2,0,1:T(8,128)(2,1)S(1)}, u32[]{:S(2)}, u32[]{:S(2)}) %collective-permute-start.3) | collective-permute-done | bytes 786464 | tf_op jit(solution)/shard_map/ppermute | solution.py:72
  88.3 0.6 convolution_bitcast_fusion.3
  88.9 0.2 pad_maximum_fusion
  89.1 2.1 %gather_fusion.1 = f32[4,3,128,3,128]{4,2,3,1,0:T(8,128)} fusion(f32[4,3,128,3,128]{4,2,3,1,0:T(8,128)S(1)} %pad_maximum_fusion, s32[1024]{0:T(1024)S(1)} %pad_clamp_fusion), kind=kCustom, calls=%fused_computation.1 | custom fusion | bytes 4718608 | tf_op jit(solution)/shard_map/gather | solution.py:83
  91.2 1.8 %fusion.28 = (f32[1,128,3,4,128]{4,1,2,0,3:T(8,128)S(1)}, f32[1,128,3,4,128]{4,1,2,0,3:T(8,128)S(1)}, f32[1,128,3,4,128]{4,1,2,0,3:T(8,128)S(1)}) fusion(f32[3,128,3,4,128]{4,1,2,0,3:T(8,128)} %bitcast.60), kind=kLoop, calls=%fused_computation.57 | loop fusion | bytes 4718592 | tf_op jit(solution)/shard_map/slice | solution.py:85
  93.0 1.2 %copy.24 = f32[1,128,3,4,128]{1,4,3,2,0:T(8,128)} copy(f32[1,128,3,4,128]{4,1,2,0,3:T(8,128)S(1)} %get-tuple-element.7) | data formatting | bytes 1572864 | tf_op jit(solution)/shard_map/slice | solution.py:85
  94.2 1.6 %collective-permute-start.5 = (f32[128,3,512]{0,2,1:T(8,128)}, f32[128,3,512]{0,2,1:T(8,128)}, u32[]{:S(2)}, u32[]{:S(2)}) collective-permute-start(f32[128,3,512]{0,2,1:T(8,128)} %bitcast.63), channel_id=1, source_target_pairs={{0,4},{4,8},{8,12},{12,16},{16,20},{20,24},{24,28},{28,0},{1,5},{5... | collective-permute-start | bytes 2359304 | tf_op jit(solution)/shard_map/ppermute | solution.py:29
  95.8 1.1 copy.26
  97.0 0.0 collective-permute-start.6
  97.0 0.3 copy.25
  97.2 13.3 %collective-permute-done.5 = f32[128,3,512]{0,2,1:T(8,128)} collective-permute-done((f32[128,3,512]{0,2,1:T(8,128)}, f32[128,3,512]{0,2,1:T(8,128)}, u32[]{:S(2)}, u32[]{:S(2)}) %collective-permute-start.5) | collective-permute-done | bytes 786464 | tf_op jit(solution)/shard_map/ppermute | solution.py:29
  110.5 4.6 %collective-permute-done.6 = f32[128,3,512]{0,2,1:T(8,128)} collective-permute-done((f32[128,3,512]{0,2,1:T(8,128)}, f32[128,3,512]{0,2,1:T(8,128)}, u32[]{:S(2)}, u32[]{:S(2)}) %collective-permute-start.6) | collective-permute-done | bytes 786464 | tf_op jit(solution)/shard_map/ppermute | solution.py:29
  115.1 1.5 %pad_add_fusion = f32[128,5,512]{0,2,1:T(8,128)S(1)} fusion(f32[128,3,512]{0,2,1:T(8,128)} %collective-permute-done.6, f32[128,3,512]{0,2,1:T(8,128)S(1)} %bitcast.62, f32[128,3,512]{0,2,1:T(8,128)} %collective-permute-done.5), kind=kLoop, calls=%fused_computation.12 | loop fusion | flops 655360 | bytes 3670016 | tf_op jit(solution)/shard_map/add | solution.py:87
  116.6 1.5 %copy.27 = f32[128,5,512]{2,0,1:T(8,128)} copy(f32[128,5,512]{0,2,1:T(8,128)S(1)} %pad_add_fusion) | data formatting | bytes 2621440 | tf_op jit(solution)/shard_map/add | solution.py:87
  (9 shorter events, 0.1 us)
Async XLA Ops:
  0.0 30.4 %copy-start = (bf16[8,3,128,128]{3,2,1,0:T(8,128)(2,1)S(1)}, bf16[8,3,128,128]{3,2,1,0:T(8,128)(2,1)}, u32[]{:S(2)}) copy-start(bf16[8,3,128,128]{3,2,1,0:T(8,128)(2,1)} %param.4) | copy-start | bytes 2359300
  0.0 5.3 %copy-start.1 = (s32[8,3]{0,1:T(4,128)S(1)}, s32[8,3]{0,1:T(4,128)}, u32[]{:S(2)}) copy-start(s32[8,3]{0,1:T(4,128)} %param.5) | copy-start | bytes 292
  2.6 5.4 %collective-permute-start = (bf16[256,3,128]{2,0,1:T(8,128)(2,1)S(1)}, bf16[256,3,128]{2,0,1:T(8,128)(2,1)S(1)}, u32[]{:S(2)}, u32[]{:S(2)}) collective-permute-start(bf16[256,3,128]{2,0,1:T(8,128)(2,1)S(1)} %get-tuple-element.10), channel_id=1, source_target_pairs={{0,4},{4,8},{8,12},{12,16},{16,20},{20,24},{24,28},{28,0},{1,5},{5... | collective-permute-start | bytes 589832 | tf_op jit(solution)/shard_map/ppermute | solution.py:20
  5.3 6.6 %collective-permute-start.1 = (bf16[256,3,128]{2,0,1:T(8,128)(2,1)S(1)}, bf16[256,3,128]{2,0,1:T(8,128)(2,1)S(1)}, u32[]{:S(2)}, u32[]{:S(2)}) collective-permute-start(bf16[256,3,128]{2,0,1:T(8,128)(2,1)S(1)} %get-tuple-element.11), channel_id=1, source_target_pairs={{4,0},{8,4},{12,8},{16,12},{20,16},{24,20},{28,24},{0,28},{5,1},{9... | collective-permute-start | bytes 589832 | tf_op jit(solution)/shard_map/ppermute | solution.py:21
  34.9 20.7 %collective-permute-start.2 = (bf16[1024,3,128]{2,0,1:T(8,128)(2,1)}, bf16[1024,3,128]{2,0,1:T(8,128)(2,1)S(1)}, u32[]{:S(2)}, u32[]{:S(2)}) collective-permute-start(bf16[1024,3,128]{2,0,1:T(8,128)(2,1)} %copy.17), channel_id=1, source_target_pairs={{0,1},{1,2},{2,3},{3,0},{4,5},{5,6},{6,7},{7,4},{8,9},{9,10},{10,1... | collective-permute-start | bytes 2359304 | tf_op jit(solution)/shard_map/ppermute | solution.py:72
  36.6 36.3 %collective-permute-start.4 = (bf16[1024,3,128]{2,0,1:T(8,128)(2,1)}, bf16[1024,3,128]{2,0,1:T(8,128)(2,1)}, u32[]{:S(2)}, u32[]{:S(2)}) collective-permute-start(bf16[1024,3,128]{2,0,1:T(8,128)(2,1)} %copy.17), channel_id=1, source_target_pairs={{0,3},{1,0},{2,1},{3,2},{4,7},{5,4},{6,5},{7,6},{8,11},{9,8},{10,9... | collective-permute-start | bytes 2359304 | tf_op jit(solution)/shard_map/ppermute | solution.py:73
  55.6 32.7 %collective-permute-start.3 = (bf16[1024,3,128]{2,0,1:T(8,128)(2,1)S(1)}, bf16[1024,3,128]{2,0,1:T(8,128)(2,1)S(1)}, u32[]{:S(2)}, u32[]{:S(2)}) collective-permute-start(bf16[1024,3,128]{2,0,1:T(8,128)(2,1)S(1)} %collective-permute-done.2), channel_id=1, source_target_pairs={{0,1},{1,2},{2,3},{3,0},{4,5},{5,6},{6,7},{7,4},{8,9},{9,10},{10,1... | collective-permute-start | bytes 2359304 | tf_op jit(solution)/shard_map/ppermute | solution.py:72
  94.2 16.3 %collective-permute-start.5 = (f32[128,3,512]{0,2,1:T(8,128)}, f32[128,3,512]{0,2,1:T(8,128)}, u32[]{:S(2)}, u32[]{:S(2)}) collective-permute-start(f32[128,3,512]{0,2,1:T(8,128)} %bitcast.63), channel_id=1, source_target_pairs={{0,4},{4,8},{8,12},{12,16},{16,20},{20,24},{24,28},{28,0},{1,5},{5... | collective-permute-start | bytes 2359304 | tf_op jit(solution)/shard_map/ppermute | solution.py:29
  97.0 18.1 %collective-permute-start.6 = (f32[128,3,512]{0,2,1:T(8,128)}, f32[128,3,512]{0,2,1:T(8,128)}, u32[]{:S(2)}, u32[]{:S(2)}) collective-permute-start(f32[128,3,512]{0,2,1:T(8,128)} %bitcast.24), channel_id=1, source_target_pairs={{0,28},{4,0},{8,4},{12,8},{16,12},{20,16},{24,20},{28,24},{1,29},{... | collective-permute-start | bytes 2359304 | tf_op jit(solution)/shard_map/ppermute | solution.py:29
